TPU v7x, 32 devices: a whole 2x2x4 slice. The times are simulated.
32 devices in a mesh: groups: 2 (over x), seq: 16 (over z, y, core).
Axes of the slice: x: 2, y: 2, z: 4, core: 2. Of those that a mesh axis runs over, the one named last changes fastest.
Arguments:
- target_queries: bfloat16 [16384, 1024], P(('groups', 'seq')), parts along dimension 0, may hold values from -8 to 8
- memory_keys: bfloat16 [16384, 1024], P(('groups', 'seq')), parts along dimension 0, may hold values from -8 to 8
- memory_values: bfloat16 [16384, 1024], P(('groups', 'seq')), parts along dimension 0, may hold values from -6 to 6
- grad_output: bfloat16 [16384, 1024], P(('groups', 'seq')), parts along dimension 0, may hold values from -6 to 6
- band_start: int32 [128], P(('groups', 'seq')), parts along dimension 0, may hold values from 0 to 63, as said below
- band_end: int32 [128], P(('groups', 'seq')), parts along dimension 0, may hold values from 4 to 64, as said below
Outputs:
- attended: bfloat16 [16384, 1024], P(('groups', 'seq')), parts along dimension 0
- grad_queries: bfloat16 [16384, 1024], P(('groups', 'seq')), parts along dimension 0
- grad_keys: bfloat16 [16384, 1024], P(('groups', 'seq')), parts along dimension 0
- grad_values: bfloat16 [16384, 1024], P(('groups', 'seq')), parts along dimension 0
There are 2 independent parts, one for each index of `groups`. A program takes and returns all parts, laid end to end along the dimension named above; each array names one. Nothing has to cross between parts.
Inputs may be any that keep to these rules, and one draw needn't show every extreme that they name: band_start never falls as the target block b grows, and band_start[b] lies between b - 3 and b. band_end never falls as b grows, and band_end[b] - band_start[b] lies between 1 and 4; the difference 4 occurs in every draw.
All inputs are finite; a program needn't handle non-finite values.
Results may differ from a plain program's by a relative error of at most 0.024.
Values may be sent and summed in bfloat16 or wider, within the bound.
No kernel may reach another device: no remote copies, remote signals or barrier semaphores. Data moves between devices by JAX's collectives and lax.ppermute only.
A program may use at most 128 MiB of HBM per device.

v0:
```python
import functools
import math

import jax
import jax.numpy as jnp
from jax import lax
from jax.experimental import pallas as pl
from jax.experimental.pallas import tpu as pltpu
from jax.sharding import PartitionSpec as P

H = 16
BLOCK = 128
MAX_BAND = 4
REACH = MAX_BAND - 1
SLOTS = 2
HEADER = 16
PIECES = (2, 4, 2)
VMEM_LIMIT = 28 * 1024 * 1024
SMALL_LIMIT = 12 * 1024 * 1024
PACK_LIMIT = 56 * 1024 * 1024
SETTLE_WEIGHT = 8

ANY = pl.BlockSpec(memory_space=pl.ANY)
SMEM = pl.BlockSpec(memory_space=pltpu.SMEM)


def rows(block, count=1):
    if isinstance(block, int):
        return pl.ds(block * BLOCK, count * BLOCK)
    return pl.ds(pl.multiple_of(block * BLOCK, BLOCK), count * BLOCK)


def position(blocks):
    index = lax.axis_index("seq")
    return index * blocks, lax.rem(index, 2) == 1


def run_copies(copies):
    for copy in copies:
        copy.start()
    for copy in copies:
        copy.wait()


def moved_up(starts, ends, first, blocks):
    return ends[blocks - 1] == first + blocks + REACH


def moved_down(starts, ends, first):
    return starts[0] == first - REACH


def edge(blocks, above, up, down):
    near = jnp.where(above, blocks - 1, 0)
    far = jnp.where(above, blocks - 2, 1)
    return near, far, (above & up) | (jnp.logical_not(above) & down)


def gather(side, cols, q, k, v, g, target, sem):
    near, far, moved = side

    def copy(source, block, part):
        return pltpu.make_async_copy(source.at[rows(block), cols], target.at[rows(part)], sem(part))

    always = [copy(k, near, 0), copy(v, near, 1)]
    goes = [copy(q, near, 2), copy(g, near, 3)]
    stays = [copy(k, far, 2), copy(v, far, 3)]
    for c in always:
        c.start()

    @pl.when(moved)
    def _():
        for c in goes:
            c.start()

    @pl.when(jnp.logical_not(moved))
    def _():
        for c in stays:
            c.start()

    return always + stays


def pack_kernel(blocks, windows, starts, ends, q, k, v, g, *rest):
    count = len(windows)
    messages, stages, sem = rest[-2 * count - 1 : -count - 1], rest[-count - 1 : -1], rest[-1]
    first, is_odd = position(blocks)
    up = moved_up(starts, ends, first, blocks)
    down = moved_down(starts, ends, first)
    up_value = jnp.where(up, MAX_BAND, 0)
    down_value = jnp.where(down, ends[0] - starts[0], 0)
    waits, values = [], []
    for index, (low, width, _, intra) in enumerate(windows):
        above = jnp.logical_not(is_odd) if intra else is_odd
        side = edge(blocks, above, up, down)
        at = lambda part, index=index: sem.at[index * 5 + part]
        waits.append(gather(side, pl.ds(low, width), q, k, v, g, stages[index], at))
        values.append(jnp.where(above, up_value, down_value))
    sends = []
    for index, (_, width, header, _) in enumerate(windows):
        if header:
            stages[index][pl.ds(2 * SLOTS * BLOCK, HEADER)] = jnp.full(
                (HEADER, width), values[index].astype(jnp.float32)
            ).astype(stages[index].dtype)
        for c in waits[index]:
            c.wait()
        sends.append(pltpu.make_async_copy(stages[index], messages[index], sem.at[index * 5 + 4]))
        sends[-1].start()
    for c in sends:
        c.wait()


def pack(name, blocks, windows, starts, ends, q, k, v, g, *after):
    shapes = tuple(
        jax.ShapeDtypeStruct((2 * SLOTS * BLOCK + (HEADER if header else 0), width), q.dtype)
        for _, width, header, _ in windows
    )
    return pl.pallas_call(
        functools.partial(pack_kernel, blocks, windows),
        out_shape=shapes,
        in_specs=[SMEM] * 2 + [ANY] * (4 + len(after)),
        out_specs=(ANY,) * len(shapes),
        scratch_shapes=[pltpu.VMEM(shape.shape, q.dtype) for shape in shapes]
        + [pltpu.SemaphoreType.DMA((5 * len(shapes),))],
        compiler_params=pltpu.CompilerParams(vmem_limit_bytes=PACK_LIMIT),
        cost_estimate=pl.CostEstimate(
            flops=0, transcendentals=0, bytes_accessed=sum(4 * math.prod(shape.shape) for shape in shapes)
        ),
        name=name,
    )(starts, ends, q, k, v, g, *after)


def attend_pairs(count, head_dim, pairs, q_row, k_row, kb, vb, qb, gb, dk, dv, ob, dqb):
    dtype = kb.dtype
    scale = 1.0 / math.sqrt(head_dim)
    window = pl.ds(k_row, count * BLOCK)
    block = pl.ds(q_row, BLOCK)
    left = lax.broadcasted_iota(jnp.int32, (BLOCK, 2 * head_dim), 1) < head_dim
    zero = jnp.zeros((BLOCK, 2 * head_dim), dtype)
    by_row = (((1,), (1,)), ((), ()))
    by_key = (((0,), (0,)), ((), ()))
    plain = (((1,), (0,)), ((), ()))
    dot = functools.partial(lax.dot_general, preferred_element_type=jnp.float32)

    def split(x):
        return jnp.concatenate([jnp.where(left, x, zero), jnp.where(left, zero, x)], axis=0)

    def diagonal(x):
        return jnp.concatenate([x[:head_dim, :BLOCK], x[head_dim:, BLOCK:]], axis=0).T.astype(dtype)

    fronts = []
    for pair in range(pairs):
        lanes = pl.ds(pair * 2 * head_dim, 2 * head_dim)
        q = split(qb[block, lanes] * jnp.asarray(scale, dtype))
        g = split(gb[block, lanes])
        keys, values = kb[window, lanes], vb[window, lanes]
        fronts.append((lanes, q, g, keys, values, dot(keys, q, by_row), dot(values, g, by_row)))
    middles = []
    for lanes, q, g, keys, values, scores, grad_probs in fronts:
        weights = jnp.exp(scores - jnp.max(scores, axis=0, keepdims=True))
        total = 1.0 / jnp.sum(weights, axis=0, keepdims=True)
        row_dot = jnp.sum(weights * grad_probs, axis=0, keepdims=True) * total
        probs = weights * total
        middles.append((probs.astype(dtype), (probs * (grad_probs - row_dot)).astype(dtype)))
    for (lanes, q, g, keys, values, _, _), (probs, grad_scores) in zip(fronts, middles):
        out = dot(values, probs, by_key)
        grad_q = dot(keys, grad_scores, by_key) * scale
        add_v = dot(probs, g, plain)
        add_k = dot(grad_scores, q, plain)
        ob[block, lanes] = diagonal(out)
        dqb[block, lanes] = diagonal(grad_q)
        dv[window, lanes] += add_v
        dk[window, lanes] += add_k


def attend_kernel(
    blocks, low_col, width, inter_row, intra_col, forward_col, head_dim,
    starts, ends, q, k, v, g, inter, intra, inter_head, intra_head, *rest
):
    attended, grad_q, back_intra, back_inter, grad_k, grad_v = rest[-18:-12]
    kb, vb, qb, gb, dk, dv, ob, dqb, low, head, ahead, sem = rest[-12:]
    first, is_odd = position(blocks)
    cols = pl.ds(low_col, width)
    own = rows(SLOTS, blocks)
    make = pltpu.make_async_copy
    note = pl.ds(2 * SLOTS * BLOCK, HEADER)
    heads = [
        make(inter_head.at[note, pl.ds(0, BLOCK)], head.at[0], sem.at[0]),
        make(intra_head.at[note, pl.ds(0, BLOCK)], head.at[1], sem.at[1]),
    ]
    loads = [
        make(k.at[:, cols], kb.at[own], sem.at[2]),
        make(v.at[:, cols], vb.at[own], sem.at[3]),
        make(q.at[:, cols], qb.at[rows(1, blocks)], sem.at[4]),
        make(g.at[:, cols], gb.at[rows(1, blocks)], sem.at[5]),
    ]
    for c in heads + loads:
        c.start()
    for c in heads:
        c.wait()
    up = moved_up(starts, ends, first, blocks)
    down = moved_down(starts, ends, first)
    onward = []
    if forward_col is not None:
        onward = gather(
            edge(blocks, is_odd, up, down), pl.ds(forward_col, width), q, k, v, g, ahead, lambda i: sem.at[14 + i]
        )
    from_inter = jnp.max(head[0].astype(jnp.float32)).astype(jnp.int32)
    from_intra = jnp.max(head[1].astype(jnp.float32)).astype(jnp.int32)
    below_span = jnp.where(is_odd, from_intra, from_inter)
    above_span = jnp.where(is_odd, from_inter, from_intra)

    near_below, far_below = SLOTS - 1, SLOTS - 2
    near_above, far_above = SLOTS + blocks, SLOTS + blocks + 1
    base = 6

    def arrive(message, near, far, target, span, slot):
        at = lambda i: sem.at[base + slot * 4 + i]
        always = [make(message(0), kb.at[rows(near)], at(0)), make(message(1), vb.at[rows(near)], at(1))]
        moved = [make(message(2), qb.at[rows(target)], at(2)), make(message(3), gb.at[rows(target)], at(3))]
        stays = [make(message(2), kb.at[rows(far)], at(2)), make(message(3), vb.at[rows(far)], at(3))]
        for c in always:
            c.start()

        @pl.when(span > 0)
        def _():
            for c in moved:
                c.start()

        @pl.when(span == 0)
        def _():
            for c in stays:
                c.start()

        return always + stays

    inter_near = jnp.where(is_odd, near_above, near_below)
    inter_far = jnp.where(is_odd, far_above, far_below)
    inter_target = jnp.where(is_odd, blocks + 1, 0)
    intra_near = jnp.where(is_odd, near_below, near_above)
    intra_far = jnp.where(is_odd, far_below, far_above)
    intra_target = jnp.where(is_odd, 0, blocks + 1)
    loads += arrive(lambda i: inter.at[pl.ds(inter_row + i * BLOCK, BLOCK)], inter_near, inter_far, inter_target, from_inter, 0)
    columns = pl.ds(intra_col, width)
    loads += arrive(lambda i: intra.at[rows(i), columns], intra_near, intra_far, intra_target, from_intra, 1)
    dk[...] = jnp.zeros_like(dk)
    dv[...] = jnp.zeros_like(dv)
    for c in loads:
        c.wait()
    back = pl.ds(0, 2 * SLOTS * BLOCK)
    for c in onward:
        c.wait()
    if onward:
        onward = [make(ahead, back_inter.at[pl.ds(2 * SLOTS * BLOCK, 2 * SLOTS * BLOCK)], sem.at[14])]
        onward[0].start()

    def task(index, carry):
        mine = jnp.clip(index - 1, 0, blocks - 1)
        lower, upper = index == 0, index == blocks + 1
        span = ends[mine] - starts[mine]
        gone = ((index == 1) & down) | ((index == blocks) & up)
        span = jnp.where(gone, 0, span)
        span = jnp.where(lower, below_span, jnp.where(upper, above_span, span))
        window = starts[mine] - first + SLOTS
        window = jnp.where(lower, near_below, jnp.where(upper, near_above - REACH, window))
        q_row = pl.multiple_of(index * BLOCK, BLOCK)
        k_row = pl.multiple_of(window * BLOCK, BLOCK)
        for size in range(1, MAX_BAND + 1):

            @pl.when(span == size)
            def _():
                attend_pairs(
                    size, head_dim, width // (2 * head_dim), q_row, k_row, kb, vb, qb, gb, dk, dv, ob, dqb
                )

        return carry

    lax.fori_loop(0, blocks + 2, task, 0)

    def leave(target, near, far, block, span, slot):
        low[slot, rows(0)] = dk[rows(near)].astype(low.dtype)
        low[slot, rows(1)] = dv[rows(near)].astype(low.dtype)

        @pl.when(span > 0)
        def _():
            low[slot, rows(2)] = ob[rows(block)]
            low[slot, rows(3)] = dqb[rows(block)]

        @pl.when(span == 0)
        def _():
            low[slot, rows(2)] = dk[rows(far)].astype(low.dtype)
            low[slot, rows(3)] = dv[rows(far)].astype(low.dtype)

        c = make(low.at[slot], target, sem.at[slot])
        c.start()
        return c

    stores = onward + [leave(back_inter.at[back], inter_near, inter_far, inter_target, from_inter, 0)]
    stores += [
        make(ob.at[rows(1, blocks)], attended.at[:, cols], sem.at[2]),
        make(dqb.at[rows(1, blocks)], grad_q.at[:, cols], sem.at[3]),
        make(dk.at[own], grad_k, sem.at[4]),
        make(dv.at[own], grad_v, sem.at[5]),
    ]
    for c in stores[-4:]:
        c.start()
    stores.append(leave(back_intra, intra_near, intra_far, intra_target, from_intra, 1))
    for c in stores:
        c.wait()


def attend(name, blocks, low_col, width, offsets, head_dim, starts, ends, q, k, v, g, messages, outs):
    inter_row, intra_col, forward_col = offsets
    low, high = q.dtype, jnp.float32
    message = 2 * SLOTS * BLOCK
    whole = jax.ShapeDtypeStruct(q.shape, low)
    back = jax.ShapeDtypeStruct((message, width), low)
    joint = back if forward_col is None else jax.ShapeDtypeStruct((2 * message, width), low)
    total = jax.ShapeDtypeStruct((blocks * BLOCK, width), high)
    sources, targets = (blocks + 2 * SLOTS) * BLOCK, (blocks + 2) * BLOCK
    pairs = blocks * MAX_BAND * (width // (2 * head_dim))
    return pl.pallas_call(
        functools.partial(attend_kernel, blocks, low_col, width, inter_row, intra_col, forward_col, head_dim),
        out_shape=(whole, whole, back, joint, total, total),
        in_specs=[SMEM] * 2 + [ANY] * (8 + len(outs)),
        out_specs=(ANY,) * 6,
        input_output_aliases={10 + i: i for i in range(len(outs))},
        scratch_shapes=[
            pltpu.VMEM((sources, width), low),
            pltpu.VMEM((sources, width), low),
            pltpu.VMEM((targets, width), low),
            pltpu.VMEM((targets, width), low),
            pltpu.VMEM((sources, width), high),
            pltpu.VMEM((sources, width), high),
            pltpu.VMEM((targets, width), low),
            pltpu.VMEM((targets, width), low),
            pltpu.VMEM((2, message, width), low),
            pltpu.VMEM((2, HEADER, BLOCK), low),
            pltpu.VMEM((message, width), low),
            pltpu.SemaphoreType.DMA((18,)),
        ],
        compiler_params=pltpu.CompilerParams(vmem_limit_bytes=VMEM_LIMIT),
        cost_estimate=pl.CostEstimate(
            flops=4 * pairs * 12 * BLOCK * 2 * BLOCK * BLOCK, transcendentals=pairs * 2 * BLOCK * BLOCK,
            bytes_accessed=16 * blocks * BLOCK * width,
        ),
        name=name,
    )(starts, ends, q, k, v, g, *messages, *outs)


def settle_kernel(blocks, parts, starts, ends, *refs):
    count = len(parts)
    totals, messages = refs[: 2 * count], refs[2 * count : 3 * count]
    attended, grad_q, out_k, out_v = refs[-3 * count - 5 : -3 * count - 1]
    landed, sums = refs[-3 * count - 1 : -2 * count - 1], refs[-2 * count - 1 : -count - 1]
    stages, sem = refs[-count - 1 : -1], refs[-1]
    first, is_odd = position(blocks)
    up = moved_up(starts, ends, first, blocks)
    down = moved_down(starts, ends, first)
    make = pltpu.make_async_copy
    sides = [edge(blocks, jnp.logical_not(is_odd) if intra else is_odd, up, down) for _, _, intra in parts]
    loads = []
    for i in range(count):
        near, far, _ = sides[i]
        loads.append([
            make(messages[i].at[pl.ds(0, 2 * SLOTS * BLOCK)], landed[i], sem.at[i, 0]),
            make(totals[2 * i].at[rows(near)], sums[i].at[rows(0)], sem.at[i, 1]),
            make(totals[2 * i + 1].at[rows(near)], sums[i].at[rows(1)], sem.at[i, 2]),
            make(totals[2 * i].at[rows(far)], sums[i].at[rows(2)], sem.at[i, 3]),
            make(totals[2 * i + 1].at[rows(far)], sums[i].at[rows(3)], sem.at[i, 4]),
        ])
        for c in loads[-1]:
            c.start()
    stores = []
    for i, (low_col, width, _) in enumerate(parts):
        cols = pl.ds(low_col, width)
        near, far, moved = sides[i]
        keep = jnp.logical_not(moved)
        for c in loads[i]:
            c.wait()
        for half in range(2):
            came = landed[i][rows(2 * half, 2)].astype(jnp.float32)
            if half:
                came = jnp.where(keep, came, jnp.zeros_like(came))
            stages[i][rows(2 * half, 2)] = (sums[i][rows(2 * half, 2)] + came).astype(stages[i].dtype)
            block = far if half else near
            stores += [
                make(stages[i].at[rows(2 * half)], out_k.at[rows(block), cols], sem.at[i, 2 * half]),
                make(stages[i].at[rows(2 * half + 1)], out_v.at[rows(block), cols], sem.at[i, 2 * half + 1]),
            ]
            for c in stores[-2:]:
                c.start()

        @pl.when(moved)
        def _():
            run_copies([
                make(landed[i].at[rows(2)], attended.at[rows(near), cols], sem.at[i, 4]),
                make(landed[i].at[rows(3)], grad_q.at[rows(near), cols], sem.at[i, 5]),
            ])

    for c in stores:
        c.wait()


def settle(name, blocks, parts, starts, ends, totals, messages, outs):
    low = outs[0].dtype
    whole = jax.ShapeDtypeStruct(outs[0].shape, low)
    count = len(parts)
    shapes = [(2 * SLOTS * BLOCK, width) for _, width, _ in parts]
    base = 2 + 3 * count
    return pl.pallas_call(
        functools.partial(settle_kernel, blocks, parts),
        out_shape=(whole,) * 4,
        in_specs=[SMEM] * 2 + [ANY] * (3 * count + len(outs)),
        out_specs=(ANY,) * 4,
        input_output_aliases={base + i: i for i in range(len(outs))},
        scratch_shapes=[pltpu.VMEM(shape, low) for shape in shapes]
        + [pltpu.VMEM(shape, jnp.float32) for shape in shapes]
        + [pltpu.VMEM(shape, low) for shape in shapes]
        + [pltpu.SemaphoreType.DMA((count, 6))],
        compiler_params=pltpu.CompilerParams(vmem_limit_bytes=SMALL_LIMIT),
        cost_estimate=pl.CostEstimate(
            flops=0, transcendentals=0, bytes_accessed=sum(SETTLE_WEIGHT * math.prod(shape) for shape in shapes)
        ),
        name=name,
    )(starts, ends, *totals, *messages, *outs)


def body(q, k, v, g, starts, ends):
    shard_rows, model_width = q.shape
    blocks = shard_rows // BLOCK
    head_dim = model_width // H
    count = lax.axis_size("seq")
    across = [(i, i + 1) for i in range(1, count - 1, 2)] + [(i + 1, i) for i in range(1, count - 1, 2)]
    inside = [(i, i ^ 1) for i in range(count)]
    pieces, low_col = [], 0
    for pairs in PIECES:
        pieces.append((low_col, pairs * 2 * head_dim))
        low_col += pairs * 2 * head_dim

    first, last = pieces[0], len(pieces) - 1
    rest_col = first[1]
    swap = lambda x, pairs: lax.ppermute(x, "seq", pairs)
    inter, intra = pack("pack0", blocks, [(*first, True, False), (*first, True, True)], starts, ends, q, k, v, g)
    heads = (swap(inter, across), swap(intra, inside))
    inter, intra = pack(
        "pack1", blocks, [(*pieces[1], False, False), (rest_col, model_width - rest_col, False, True)],
        starts, ends, q, k, v, g, inter,
    )
    arrived = [heads, (swap(inter, across), swap(intra, inside))]

    outs, totals, returned = (), [], []
    for i, piece in enumerate(pieces):
        if i > 1:
            arrived.append((returned[i - 2][0], arrived[1][1]))
        inter_row = 2 * SLOTS * BLOCK if i > 1 else 0
        intra_col = piece[0] - rest_col if i else 0
        forward_col = pieces[i + 2][0] if i + 2 <= last else None
        results = attend(
            f"attend{i}", blocks, *piece, (inter_row, intra_col, forward_col), head_dim, starts, ends, q, k, v, g,
            (*arrived[i], *heads), outs,
        )
        outs = results[:2]
        returned.append((swap(results[3], across), swap(results[2], inside)))
        totals.append(results[4:])
    for name, members in (("settle_a", range(last)), ("settle_b", (last,))):
        parts = [(*pieces[i], inner) for i in members for inner in (False, True)]
        outs = settle(
            name, blocks, parts, starts, ends, [x for i in members for _ in range(2) for x in totals[i]],
            [x for i in members for x in returned[i]], outs,
        )
    return outs


def solution(mesh):
    spec = P(("groups", "seq"), None)
    flat = P(("groups", "seq"))
    return jax.shard_map(
        body,
        mesh=mesh,
        in_specs=(spec, spec, spec, spec, flat, flat),
        out_specs=(spec, spec, spec, spec),
        check_vma=False,
    )
```

profile of v0, /device:TPU:6, one launch (start us, length us, event | category | flops | bytes accessed | tf_op | source)
XLA Modules:
  0.0 63.7 jit_solution(9003798218662787961)
XLA Ops:
  0.6 2.5 %pack0.1 = (bf16[528,256]{1,0:T(8,128)(2,1)}, bf16[528,256]{1,0:T(8,128)(2,1)}) custom-call(s32[4]{0:T(128)} %starts.13, s32[4]{0:T(128)} %ends.13, bf16[512,1024]{1,0:T(8,128)(2,1)} %q.9, bf16[512,1024]{1,0:T(8,128)(2,1)} %k.9, bf16[512,1024]{1,0:T(8,128)(2,1)} %v.9, bf16[512,1024]{1,0:T(8,128)(2,1)} %g.9), custom_call_target="tpu_custom_call" | custom-call | bytes 1081344 | tf_op jit(solution)/shard_map/pack0/pallas_call | solution.py:118
  3.2 0.1 collective-permute-start.1
  3.3 0.0 copy-start
  3.3 0.0 copy-start.1
  3.3 0.0 copy-start.2
  3.3 0.0 copy-start.3
  3.3 2.7 %collective-permute-start = (bf16[528,256]{1,0:T(8,128)(2,1)}, bf16[528,256]{1,0:T(8,128)(2,1)S(1)}, u32[]{:S(2)}, u32[]{:S(2)}) collective-permute-start(bf16[528,256]{1,0:T(8,128)(2,1)} %get-tuple-element.30.rest_0_), channel_id=1, source_target_pairs={{1,2},{3,4},{5,6},{7,8},{9,10},{11,12},{13,14},{2,1},{4,3},{6,5},{... | collective-permute-start | bytes 811016 | tf_op jit(solution)/shard_map/ppermute | solution.py:443
  6.1 3.0 %pack1.1 = (bf16[512,512]{1,0:T(8,128)(2,1)}, bf16[512,768]{1,0:T(8,128)(2,1)}) custom-call(s32[4]{0:T(128)} %starts.13, s32[4]{0:T(128)} %ends.13, bf16[512,1024]{1,0:T(8,128)(2,1)} %q.9, bf16[512,1024]{1,0:T(8,128)(2,1)} %k.9, bf16[512,1024]{1,0:T(8,128)(2,1)} %v.9, bf16[512,1024]{1,0:T(8,128)(2,1)} %g.9, bf16[528,256]{1,0:T(8,128)(2,1)} %get-tuple-element.30.rest_0_), custom_call_target="tpu_custom_call" | custom-call | bytes 2621440 | tf_op jit(solution)/shard_map/pack1/pallas_call | solution.py:118
  9.1 0.0 copy-start.4
  9.1 0.0 copy-start.5
  9.1 1.1 %collective-permute-start.3 = (bf16[512,768]{1,0:T(8,128)(2,1)}, bf16[512,768]{1,0:T(8,128)(2,1)S(1)}, u32[]{:S(2)}, u32[]{:S(2)}) collective-permute-start(bf16[512,768]{1,0:T(8,128)(2,1)} %get-tuple-element.33), channel_id=1, source_target_pairs={{0,1},{1,0},{2,3},{3,2},{4,5},{5,4},{6,7},{7,6},{8,9},{9,8},{10,11... | collective-permute-start | bytes 2359304 | tf_op jit(solution)/shard_map/ppermute | solution.py:443
  10.2 2.0 %collective-permute-start.4 = (bf16[512,512]{1,0:T(8,128)(2,1)}, bf16[512,512]{1,0:T(8,128)(2,1)S(1)}, u32[]{:S(2)}, u32[]{:S(2)}) collective-permute-start(bf16[512,512]{1,0:T(8,128)(2,1)} %get-tuple-element.34), channel_id=1, source_target_pairs={{1,2},{3,4},{5,6},{7,8},{9,10},{11,12},{13,14},{2,1},{4,3},{6,5},{... | collective-permute-start | bytes 1572872 | tf_op jit(solution)/shard_map/ppermute | solution.py:443
  12.3 0.0 collective-permute-done.1.intra.intra_head
  12.3 2.2 %collective-permute-done.inter.inter_head = bf16[528,256]{1,0:T(8,128)(2,1)S(1)} collective-permute-done((bf16[528,256]{1,0:T(8,128)(2,1)}, bf16[528,256]{1,0:T(8,128)(2,1)S(1)}, u32[]{:S(2)}, u32[]{:S(2)}) %collective-permute-start) | collective-permute-done | bytes 270368 | tf_op jit(solution)/shard_map/ppermute | solution.py:443
  14.5 7.6 %attend0.1 = (bf16[512,1024]{1,0:T(8,128)(2,1)}, bf16[512,1024]{1,0:T(8,128)(2,1)}, bf16[512,256]{1,0:T(8,128)(2,1)S(1)}, bf16[1024,256]{1,0:T(8,128)(2,1)S(1)},...) custom-call(s32[4]{0:T(128)S(1)} %copy-done.4, s32[4]{0:T(128)S(1)} %copy-done.5, bf16[512,1024]{1,0:T(8,128)(2,1)S(1)} %copy-done, ...), custom_call_target="tpu_custom_call" | custom-call | flops 6442450944 | bytes 2097152 | tf_op jit(solution)/shard_map/attend0/pallas_call | solution.py:322
  22.2 0.1 collective-permute-start.7
  22.2 1.9 %collective-permute-start.2 = (bf16[1024,256]{1,0:T(8,128)(2,1)S(1)}, bf16[1024,256]{1,0:T(8,128)(2,1)S(1)}, u32[]{:S(2)}, u32[]{:S(2)}) collective-permute-start(bf16[1024,256]{1,0:T(8,128)(2,1)S(1)} %get-tuple-element.32), channel_id=1, source_target_pairs={{1,2},{3,4},{5,6},{7,8},{9,10},{11,12},{13,14},{2,1},{4,3},{6,5},{... | collective-permute-start | bytes 1572872 | tf_op jit(solution)/shard_map/ppermute | solution.py:443
  24.2 2.4 %collective-permute-done.4.inter = bf16[512,512]{1,0:T(8,128)(2,1)S(1)} collective-permute-done((bf16[512,512]{1,0:T(8,128)(2,1)}, bf16[512,512]{1,0:T(8,128)(2,1)S(1)}, u32[]{:S(2)}, u32[]{:S(2)}) %collective-permute-start.4) | collective-permute-done | bytes 524320 | tf_op jit(solution)/shard_map/ppermute | solution.py:443
  26.6 11.6 %attend1.1 = (bf16[512,1024]{1,0:T(8,128)(2,1)}, bf16[512,1024]{1,0:T(8,128)(2,1)}, bf16[512,512]{1,0:T(8,128)(2,1)S(1)}, bf16[512,512]{1,0:T(8,128)(2,1)S(1)}, ...) custom-call(s32[4]{0:T(128)S(1)} %copy-done.4, s32[4]{0:T(128)S(1)} %copy-done.5, ...), custom_call_target="tpu_custom_call", output_to_operand_aliasing={{0}: (10, {}), {1}: (11, {})} | custom-call | flops 12884901888 | bytes 4194304 | tf_op jit(solution)/shard_map/attend1/pallas_call | solution.py:322
  38.2 1.9 %collective-permute-start.8 = (bf16[512,512]{1,0:T(8,128)(2,1)S(1)}, bf16[512,512]{1,0:T(8,128)(2,1)S(1)}, u32[]{:S(2)}, u32[]{:S(2)}) collective-permute-start(bf16[512,512]{1,0:T(8,128)(2,1)S(1)} %get-tuple-element.48), channel_id=1, source_target_pairs={{1,2},{3,4},{5,6},{7,8},{9,10},{11,12},{13,14},{2,1},{4,3},{6,5},{... | collective-permute-start | bytes 1572872 | tf_op jit(solution)/shard_map/ppermute | solution.py:443
  40.1 0.1 collective-permute-start.9
  40.2 0.0 collective-permute-done.2.inter.refs_8_
  40.2 7.4 %attend2.1 = (bf16[512,1024]{1,0:T(8,128)(2,1)}, bf16[512,1024]{1,0:T(8,128)(2,1)}, bf16[512,256]{1,0:T(8,128)(2,1)S(1)}, bf16[512,256]{1,0:T(8,128)(2,1)S(1)}, ...) custom-call(s32[4]{0:T(128)S(1)} %copy-done.4, s32[4]{0:T(128)S(1)} %copy-done.5, ...), custom_call_target="tpu_custom_call", output_to_operand_aliasing={{0}: (10, {}), {1}: (11, {})} | custom-call | flops 6442450944 | bytes 2097152 | tf_op jit(solution)/shard_map/attend2/pallas_call | solution.py:322
  47.7 3.4 %collective-permute-start.5 = (bf16[512,256]{1,0:T(8,128)(2,1)S(1)}, bf16[512,256]{1,0:T(8,128)(2,1)S(1)}, u32[]{:S(2)}, u32[]{:S(2)}) collective-permute-start(bf16[512,256]{1,0:T(8,128)(2,1)S(1)} %get-tuple-element.41), channel_id=1, source_target_pairs={{1,2},{3,4},{5,6},{7,8},{9,10},{11,12},{13,14},{2,1},{4,3},{6,5},{... | collective-permute-start | bytes 786440 | tf_op jit(solution)/shard_map/ppermute | solution.py:443
  51.1 0.1 collective-permute-start.6
  51.2 0.0 collective-permute-done.7.refs_9_
  51.2 5.9 %collective-permute-done.8.refs_10_ = bf16[512,512]{1,0:T(8,128)(2,1)S(1)} collective-permute-done((bf16[512,512]{1,0:T(8,128)(2,1)S(1)}, bf16[512,512]{1,0:T(8,128)(2,1)S(1)}, u32[]{:S(2)}, u32[]{:S(2)}) %collective-permute-start.8) | collective-permute-done | bytes 524320 | tf_op jit(solution)/shard_map/ppermute | solution.py:443
  57.1 0.0 collective-permute-done.9.refs_11_
  57.1 3.5 %settle_a.1 = (bf16[512,1024]{1,0:T(8,128)(2,1)}, bf16[512,1024]{1,0:T(8,128)(2,1)}, bf16[512,1024]{1,0:T(8,128)(2,1)}, bf16[512,1024]{1,0:T(8,128)(2,1)}) custom-call(s32[4]{0:T(128)S(1)} %copy-done.4, s32[4]{0:T(128)S(1)} %copy-done.5, f32[512,256]{1,0:T(8,128)S(1)} %get-tuple-element.43.refs_0_.refs_2_, ...), custom_call_target="tpu_custom_call", output_to_operand_aliasing={{0}: (14, {}), {1}: (15, {})} | custom-call | bytes 6291456 | tf_op jit(solution)/shard_map/settle_a/pallas_call | solution.py:411
  60.7 0.0 collective-permute-done.5.refs_4_
  60.7 0.0 collective-permute-done.6.refs_5_
  60.7 2.9 %settle_b.1 = (bf16[512,1024]{1,0:T(8,128)(2,1)}, bf16[512,1024]{1,0:T(8,128)(2,1)}, bf16[512,1024]{1,0:T(8,128)(2,1)}, bf16[512,1024]{1,0:T(8,128)(2,1)}) custom-call(s32[4]{0:T(128)S(1)} %copy-done.4, s32[4]{0:T(128)S(1)} %copy-done.5, ...), custom_call_target="tpu_custom_call", output_to_operand_aliasing={{0}: (8, {}), {1}: (9, {}), {2}: (10, {}), {3}: (11, {})} | custom-call | bytes 2097152 | tf_op jit(solution)/shard_map/settle_b/pallas_call | solution.py:411
  (7 shorter events, 0.0 us)
Async XLA Ops:
  3.2 9.1 %collective-permute-start.1 = (bf16[528,256]{1,0:T(8,128)(2,1)}, bf16[528,256]{1,0:T(8,128)(2,1)S(1)}, u32[]{:S(2)}, u32[]{:S(2)}) collective-permute-start(bf16[528,256]{1,0:T(8,128)(2,1)} %get-tuple-element.31), channel_id=1, source_target_pairs={{0,1},{1,0},{2,3},{3,2},{4,5},{5,4},{6,7},{7,6},{8,9},{9,8},{10,11... | collective-permute-start | bytes 811016 | tf_op jit(solution)/shard_map/ppermute | solution.py:443
  3.3 11.2 %copy-start = (bf16[512,1024]{1,0:T(8,128)(2,1)S(1)}, bf16[512,1024]{1,0:T(8,128)(2,1)}, u32[]{:S(2)}) copy-start(bf16[512,1024]{1,0:T(8,128)(2,1)} %q.9) | copy-start | bytes 3145732
  3.3 11.2 %copy-start.1 = (bf16[512,1024]{1,0:T(8,128)(2,1)S(1)}, bf16[512,1024]{1,0:T(8,128)(2,1)}, u32[]{:S(2)}) copy-start(bf16[512,1024]{1,0:T(8,128)(2,1)} %k.9) | copy-start | bytes 3145732
  3.3 11.2 %copy-start.2 = (bf16[512,1024]{1,0:T(8,128)(2,1)S(1)}, bf16[512,1024]{1,0:T(8,128)(2,1)}, u32[]{:S(2)}) copy-start(bf16[512,1024]{1,0:T(8,128)(2,1)} %v.9) | copy-start | bytes 3145732
  3.3 11.2 %copy-start.3 = (bf16[512,1024]{1,0:T(8,128)(2,1)S(1)}, bf16[512,1024]{1,0:T(8,128)(2,1)}, u32[]{:S(2)}) copy-start(bf16[512,1024]{1,0:T(8,128)(2,1)} %g.9) | copy-start | bytes 3145732
  3.3 11.1 %collective-permute-start = (bf16[528,256]{1,0:T(8,128)(2,1)}, bf16[528,256]{1,0:T(8,128)(2,1)S(1)}, u32[]{:S(2)}, u32[]{:S(2)}) collective-permute-start(bf16[528,256]{1,0:T(8,128)(2,1)} %get-tuple-element.30.rest_0_), channel_id=1, source_target_pairs={{1,2},{3,4},{5,6},{7,8},{9,10},{11,12},{13,14},{2,1},{4,3},{6,5},{... | collective-permute-start | bytes 811016 | tf_op jit(solution)/shard_map/ppermute | solution.py:443
  9.1 5.4 %copy-start.4 = (s32[4]{0:T(128)S(1)}, s32[4]{0:T(128)}, u32[]{:S(2)}) copy-start(s32[4]{0:T(128)} %starts.13) | copy-start | bytes 52
  9.1 5.4 %copy-start.5 = (s32[4]{0:T(128)S(1)}, s32[4]{0:T(128)}, u32[]{:S(2)}) copy-start(s32[4]{0:T(128)} %ends.13) | copy-start | bytes 52
  9.1 17.4 %collective-permute-start.3 = (bf16[512,768]{1,0:T(8,128)(2,1)}, bf16[512,768]{1,0:T(8,128)(2,1)S(1)}, u32[]{:S(2)}, u32[]{:S(2)}) collective-permute-start(bf16[512,768]{1,0:T(8,128)(2,1)} %get-tuple-element.33), channel_id=1, source_target_pairs={{0,1},{1,0},{2,3},{3,2},{4,5},{5,4},{6,7},{7,6},{8,9},{9,8},{10,11... | collective-permute-start | bytes 2359304 | tf_op jit(solution)/shard_map/ppermute | solution.py:443
  10.2 16.3 %collective-permute-start.4 = (bf16[512,512]{1,0:T(8,128)(2,1)}, bf16[512,512]{1,0:T(8,128)(2,1)S(1)}, u32[]{:S(2)}, u32[]{:S(2)}) collective-permute-start(bf16[512,512]{1,0:T(8,128)(2,1)} %get-tuple-element.34), channel_id=1, source_target_pairs={{1,2},{3,4},{5,6},{7,8},{9,10},{11,12},{13,14},{2,1},{4,3},{6,5},{... | collective-permute-start | bytes 1572872 | tf_op jit(solution)/shard_map/ppermute | solution.py:443
  22.2 29.1 %collective-permute-start.7 = (bf16[512,256]{1,0:T(8,128)(2,1)S(1)}, bf16[512,256]{1,0:T(8,128)(2,1)S(1)}, u32[]{:S(2)}, u32[]{:S(2)}) collective-permute-start(bf16[512,256]{1,0:T(8,128)(2,1)S(1)} %get-tuple-element.47), channel_id=1, source_target_pairs={{0,1},{1,0},{2,3},{3,2},{4,5},{5,4},{6,7},{7,6},{8,9},{9,8},{10,11... | collective-permute-start | bytes 786440 | tf_op jit(solution)/shard_map/ppermute | solution.py:443
  22.2 18.0 %collective-permute-start.2 = (bf16[1024,256]{1,0:T(8,128)(2,1)S(1)}, bf16[1024,256]{1,0:T(8,128)(2,1)S(1)}, u32[]{:S(2)}, u32[]{:S(2)}) collective-permute-start(bf16[1024,256]{1,0:T(8,128)(2,1)S(1)} %get-tuple-element.32), channel_id=1, source_target_pairs={{1,2},{3,4},{5,6},{7,8},{9,10},{11,12},{13,14},{2,1},{4,3},{6,5},{... | collective-permute-start | bytes 1572872 | tf_op jit(solution)/shard_map/ppermute | solution.py:443
  38.2 18.9 %collective-permute-start.8 = (bf16[512,512]{1,0:T(8,128)(2,1)S(1)}, bf16[512,512]{1,0:T(8,128)(2,1)S(1)}, u32[]{:S(2)}, u32[]{:S(2)}) collective-permute-start(bf16[512,512]{1,0:T(8,128)(2,1)S(1)} %get-tuple-element.48), channel_id=1, source_target_pairs={{1,2},{3,4},{5,6},{7,8},{9,10},{11,12},{13,14},{2,1},{4,3},{6,5},{... | collective-permute-start | bytes 1572872 | tf_op jit(solution)/shard_map/ppermute | solution.py:443
  40.1 17.0 %collective-permute-start.9 = (bf16[512,512]{1,0:T(8,128)(2,1)S(1)}, bf16[512,512]{1,0:T(8,128)(2,1)S(1)}, u32[]{:S(2)}, u32[]{:S(2)}) collective-permute-start(bf16[512,512]{1,0:T(8,128)(2,1)S(1)} %get-tuple-element.49), channel_id=1, source_target_pairs={{0,1},{1,0},{2,3},{3,2},{4,5},{5,4},{6,7},{7,6},{8,9},{9,8},{10,11... | collective-permute-start | bytes 1572872 | tf_op jit(solution)/shard_map/ppermute | solution.py:443
  47.7 13.0 %collective-permute-start.5 = (bf16[512,256]{1,0:T(8,128)(2,1)S(1)}, bf16[512,256]{1,0:T(8,128)(2,1)S(1)}, u32[]{:S(2)}, u32[]{:S(2)}) collective-permute-start(bf16[512,256]{1,0:T(8,128)(2,1)S(1)} %get-tuple-element.41), channel_id=1, source_target_pairs={{1,2},{3,4},{5,6},{7,8},{9,10},{11,12},{13,14},{2,1},{4,3},{6,5},{... | collective-permute-start | bytes 786440 | tf_op jit(solution)/shard_map/ppermute | solution.py:443
  51.1 9.6 %collective-permute-start.6 = (bf16[512,256]{1,0:T(8,128)(2,1)S(1)}, bf16[512,256]{1,0:T(8,128)(2,1)S(1)}, u32[]{:S(2)}, u32[]{:S(2)}) collective-permute-start(bf16[512,256]{1,0:T(8,128)(2,1)S(1)} %get-tuple-element.42), channel_id=1, source_target_pairs={{0,1},{1,0},{2,3},{3,2},{4,5},{5,4},{6,7},{7,6},{8,9},{9,8},{10,11... | collective-permute-start | bytes 786440 | tf_op jit(solution)/shard_map/ppermute | solution.py:443
where the time goes:
time: 63.8 us; the launch traced here: 63.7 us
  Pallas kernels  38.7 us (61%)
  starting transfers between devices  13.5 us (21%)
  waiting for transfers between devices  10.5 us (16%)
  between operations  1.01 us (2%)
    pallas_call x3, Pallas kernels, attend(): pl.pallas_call(functools.partial(attend_kernel, blocks, low_col, width, i...  26.7 us
    ppermute x10, starting transfers between devices, body(): swap = lambda x, pairs: lax.ppermute(x, 'seq', pairs)  13.5 us
    ppermute x10, waiting for transfers between devices, body(): swap = lambda x, pairs: lax.ppermute(x, 'seq', pairs)  10.5 us
    pallas_call x2, Pallas kernels, settle(): pl.pallas_call(functools.partial(settle_kernel, blocks, parts), out_shape...  6.42 us
    pallas_call x2, Pallas kernels, pack(): pl.pallas_call(functools.partial(pack_kernel, blocks, windows), out_shape...  5.57 us
  transfers between devices with their start and end apart: 10, of which 3 were waited for; matrix products, arithmetic and copies ran while one was open for 0% of the time, Pallas kernels for 52%

commit v1 on v0

--- a/solution.py
+++ b/solution.py
@@ -371,7 +371,7 @@
         ])
         for c in loads[-1]:
             c.start()
-    stores = []
+    stores, finished = [], []
     for i, (low_col, width, _) in enumerate(parts):
         cols = pl.ds(low_col, width)
         near, far, moved = sides[i]
@@ -391,12 +391,23 @@
             for c in stores[-2:]:
                 c.start()
 
+        whole = [
+            make(landed[i].at[rows(2)], attended.at[rows(near), cols], sem.at[i, 4]),
+            make(landed[i].at[rows(3)], grad_q.at[rows(near), cols], sem.at[i, 5]),
+        ]
+        finished.append((moved, whole))
+
         @pl.when(moved)
         def _():
-            run_copies([
-                make(landed[i].at[rows(2)], attended.at[rows(near), cols], sem.at[i, 4]),
-                make(landed[i].at[rows(3)], grad_q.at[rows(near), cols], sem.at[i, 5]),
-            ])
+            for c in whole:
+                c.start()
+
+    for moved, whole in finished:
+
+        @pl.when(moved)
+        def _():
+            for c in whole:
+                c.wait()
 
     for c in stores:
         c.wait()
@@ -463,11 +474,15 @@
         outs = results[:2]
         returned.append((swap(results[3], across), swap(results[2], inside)))
         totals.append(results[4:])
-    for name, members in (("settle_a", range(last)), ("settle_b", (last,))):
-        parts = [(*pieces[i], inner) for i in members for inner in (False, True)]
+    stages = (
+        [(0, False)] + [(i, True) for i in range(last + 1)],
+        *([(i, False)] for i in range(1, last + 1)),
+    )
+    for stage, members in enumerate(stages):
+        parts = [(*pieces[i], inner) for i, inner in members]
         outs = settle(
-            name, blocks, parts, starts, ends, [x for i in members for _ in range(2) for x in totals[i]],
-            [x for i in members for x in returned[i]], outs,
+            f"settle{stage}", blocks, parts, starts, ends, [x for i, _ in members for x in totals[i]],
+            [returned[i][int(inner)] for i, inner in members], outs,
         )
     return outs
 

time: 63.8 us -> 64.3 us (level)
  the two profiles are of different devices: /device:TPU:6 before, /device:TPU:19 now
where the time goes in v1:
time: 64.3 us; the launch traced here: 63.4 us
  Pallas kernels  38.9 us (60%)
  starting transfers between devices  17.4 us (27%)
  waiting for transfers between devices  6.13 us (10%)
  between operations  0.98 us (2%)
    pallas_call x3, Pallas kernels, attend(): pl.pallas_call(functools.partial(attend_kernel, blocks, low_col, width, i...  25.7 us
    ppermute x10, starting transfers between devices, body(): swap = lambda x, pairs: lax.ppermute(x, 'seq', pairs)  17.4 us
    pallas_call x3, Pallas kernels, settle(): pl.pallas_call(functools.partial(settle_kernel, blocks, parts), out_shape...  7.65 us
    ppermute x10, waiting for transfers between devices, body(): swap = lambda x, pairs: lax.ppermute(x, 'seq', pairs)  6.13 us
    pallas_call x2, Pallas kernels, pack(): pl.pallas_call(functools.partial(pack_kernel, blocks, windows), out_shape...  5.57 us
  transfers between devices with their start and end apart: 10, of which 3 were waited for; matrix products, arithmetic and copies ran while one was open for 0% of the time, Pallas kernels for 54%

profile of v1, /device:TPU:19, one launch (start us, length us, event | category | flops | bytes accessed | tf_op | source)
XLA Modules:
  0.0 63.4 jit_solution(15983430632238810043)
XLA Ops:
  0.6 2.5 %pack0.1 = (bf16[528,256]{1,0:T(8,128)(2,1)}, bf16[528,256]{1,0:T(8,128)(2,1)}) custom-call(s32[4]{0:T(128)} %starts.15, s32[4]{0:T(128)} %ends.15, bf16[512,1024]{1,0:T(8,128)(2,1)} %q.9, bf16[512,1024]{1,0:T(8,128)(2,1)} %k.9, bf16[512,1024]{1,0:T(8,128)(2,1)} %v.9, bf16[512,1024]{1,0:T(8,128)(2,1)} %g.9), custom_call_target="tpu_custom_call" | custom-call | bytes 1081344 | tf_op jit(solution)/shard_map/pack0/pallas_call | solution.py:118
  3.2 0.7 %collective-permute-start.1 = (bf16[528,256]{1,0:T(8,128)(2,1)}, bf16[528,256]{1,0:T(8,128)(2,1)S(1)}, u32[]{:S(2)}, u32[]{:S(2)}) collective-permute-start(bf16[528,256]{1,0:T(8,128)(2,1)} %get-tuple-element.35), channel_id=1, source_target_pairs={{0,1},{1,0},{2,3},{3,2},{4,5},{5,4},{6,7},{7,6},{8,9},{9,8},{10,11... | collective-permute-start | bytes 811016 | tf_op jit(solution)/shard_map/ppermute | solution.py:454
  3.9 3.3 %collective-permute-start = (bf16[528,256]{1,0:T(8,128)(2,1)}, bf16[528,256]{1,0:T(8,128)(2,1)S(1)}, u32[]{:S(2)}, u32[]{:S(2)}) collective-permute-start(bf16[528,256]{1,0:T(8,128)(2,1)} %get-tuple-element.34.rest_0_), channel_id=1, source_target_pairs={{1,2},{3,4},{5,6},{7,8},{9,10},{11,12},{13,14},{2,1},{4,3},{6,5},{... | collective-permute-start | bytes 811016 | tf_op jit(solution)/shard_map/ppermute | solution.py:454
  7.3 3.0 %pack1.1 = (bf16[512,512]{1,0:T(8,128)(2,1)}, bf16[512,768]{1,0:T(8,128)(2,1)}) custom-call(s32[4]{0:T(128)} %starts.15, s32[4]{0:T(128)} %ends.15, bf16[512,1024]{1,0:T(8,128)(2,1)} %q.9, bf16[512,1024]{1,0:T(8,128)(2,1)} %k.9, bf16[512,1024]{1,0:T(8,128)(2,1)} %v.9, bf16[512,1024]{1,0:T(8,128)(2,1)} %g.9, bf16[528,256]{1,0:T(8,128)(2,1)} %get-tuple-element.34.rest_0_), custom_call_target="tpu_custom_call" | custom-call | bytes 2621440 | tf_op jit(solution)/shard_map/pack1/pallas_call | solution.py:118
  10.3 0.0 copy-start.4
  10.3 0.0 copy-start.5
  10.3 0.4 collective-permute-start.3
  10.8 3.2 %collective-permute-start.4 = (bf16[512,512]{1,0:T(8,128)(2,1)}, bf16[512,512]{1,0:T(8,128)(2,1)S(1)}, u32[]{:S(2)}, u32[]{:S(2)}) collective-permute-start(bf16[512,512]{1,0:T(8,128)(2,1)} %get-tuple-element.38), channel_id=1, source_target_pairs={{1,2},{3,4},{5,6},{7,8},{9,10},{11,12},{13,14},{2,1},{4,3},{6,5},{... | collective-permute-start | bytes 1572872 | tf_op jit(solution)/shard_map/ppermute | solution.py:454
  14.0 0.0 collective-permute-done.1.intra.intra_head
  14.0 1.1 %collective-permute-done.inter.inter_head = bf16[528,256]{1,0:T(8,128)(2,1)S(1)} collective-permute-done((bf16[528,256]{1,0:T(8,128)(2,1)}, bf16[528,256]{1,0:T(8,128)(2,1)S(1)}, u32[]{:S(2)}, u32[]{:S(2)}) %collective-permute-start) | collective-permute-done | bytes 270368 | tf_op jit(solution)/shard_map/ppermute | solution.py:454
  15.1 0.0 copy-done
  15.1 0.0 copy-done.1
  15.1 7.4 %attend0.1 = (bf16[512,1024]{1,0:T(8,128)(2,1)}, bf16[512,1024]{1,0:T(8,128)(2,1)}, bf16[512,256]{1,0:T(8,128)(2,1)S(1)}, bf16[1024,256]{1,0:T(8,128)(2,1)S(1)},...) custom-call(s32[4]{0:T(128)S(1)} %copy-done.4, s32[4]{0:T(128)S(1)} %copy-done.5, bf16[512,1024]{1,0:T(8,128)(2,1)S(1)} %copy-done, ...), custom_call_target="tpu_custom_call" | custom-call | flops 6442450944 | bytes 2097152 | tf_op jit(solution)/shard_map/attend0/pallas_call | solution.py:322
  22.6 0.5 collective-permute-start.7
  23.1 1.9 %collective-permute-start.2 = (bf16[1024,256]{1,0:T(8,128)(2,1)S(1)}, bf16[1024,256]{1,0:T(8,128)(2,1)S(1)}, u32[]{:S(2)}, u32[]{:S(2)}) collective-permute-start(bf16[1024,256]{1,0:T(8,128)(2,1)S(1)} %get-tuple-element.36), channel_id=1, source_target_pairs={{1,2},{3,4},{5,6},{7,8},{9,10},{11,12},{13,14},{2,1},{4,3},{6,5},{... | collective-permute-start | bytes 1572872 | tf_op jit(solution)/shard_map/ppermute | solution.py:454
  25.0 2.1 %collective-permute-done.4.inter = bf16[512,512]{1,0:T(8,128)(2,1)S(1)} collective-permute-done((bf16[512,512]{1,0:T(8,128)(2,1)}, bf16[512,512]{1,0:T(8,128)(2,1)S(1)}, u32[]{:S(2)}, u32[]{:S(2)}) %collective-permute-start.4) | collective-permute-done | bytes 524320 | tf_op jit(solution)/shard_map/ppermute | solution.py:454
  27.1 0.0 collective-permute-done.3.intra
  27.1 11.1 %attend1.1 = (bf16[512,1024]{1,0:T(8,128)(2,1)}, bf16[512,1024]{1,0:T(8,128)(2,1)}, bf16[512,512]{1,0:T(8,128)(2,1)S(1)}, bf16[512,512]{1,0:T(8,128)(2,1)S(1)}, ...) custom-call(s32[4]{0:T(128)S(1)} %copy-done.4, s32[4]{0:T(128)S(1)} %copy-done.5, ...), custom_call_target="tpu_custom_call", output_to_operand_aliasing={{0}: (10, {}), {1}: (11, {})} | custom-call | flops 12884901888 | bytes 4194304 | tf_op jit(solution)/shard_map/attend1/pallas_call | solution.py:322
  38.2 1.9 %collective-permute-start.6 = (bf16[512,512]{1,0:T(8,128)(2,1)S(1)}, bf16[512,512]{1,0:T(8,128)(2,1)S(1)}, u32[]{:S(2)}, u32[]{:S(2)}) collective-permute-start(bf16[512,512]{1,0:T(8,128)(2,1)S(1)} %get-tuple-element.48), channel_id=1, source_target_pairs={{1,2},{3,4},{5,6},{7,8},{9,10},{11,12},{13,14},{2,1},{4,3},{6,5},{... | collective-permute-start | bytes 1572872 | tf_op jit(solution)/shard_map/ppermute | solution.py:454
  40.1 1.7 %collective-permute-start.8 = (bf16[512,512]{1,0:T(8,128)(2,1)S(1)}, bf16[512,512]{1,0:T(8,128)(2,1)S(1)}, u32[]{:S(2)}, u32[]{:S(2)}) collective-permute-start(bf16[512,512]{1,0:T(8,128)(2,1)S(1)} %get-tuple-element.52), channel_id=1, source_target_pairs={{0,1},{1,0},{2,3},{3,2},{4,5},{5,4},{6,7},{7,6},{8,9},{9,8},{10,11... | collective-permute-start | bytes 1572872 | tf_op jit(solution)/shard_map/ppermute | solution.py:454
  41.8 0.0 collective-permute-done.2.inter.refs_8_
  41.8 7.2 %attend2.1 = (bf16[512,1024]{1,0:T(8,128)(2,1)}, bf16[512,1024]{1,0:T(8,128)(2,1)}, bf16[512,256]{1,0:T(8,128)(2,1)S(1)}, bf16[512,256]{1,0:T(8,128)(2,1)S(1)}, ...) custom-call(s32[4]{0:T(128)S(1)} %copy-done.4, s32[4]{0:T(128)S(1)} %copy-done.5, ...), custom_call_target="tpu_custom_call", output_to_operand_aliasing={{0}: (10, {}), {1}: (11, {})} | custom-call | flops 6442450944 | bytes 2097152 | tf_op jit(solution)/shard_map/attend2/pallas_call | solution.py:322
  49.0 1.7 %collective-permute-start.9 = (bf16[512,256]{1,0:T(8,128)(2,1)S(1)}, bf16[512,256]{1,0:T(8,128)(2,1)S(1)}, u32[]{:S(2)}, u32[]{:S(2)}) collective-permute-start(bf16[512,256]{1,0:T(8,128)(2,1)S(1)} %get-tuple-element.53), channel_id=1, source_target_pairs={{0,1},{1,0},{2,3},{3,2},{4,5},{5,4},{6,7},{7,6},{8,9},{9,8},{10,11... | collective-permute-start | bytes 786440 | tf_op jit(solution)/shard_map/ppermute | solution.py:454
  50.7 1.9 %collective-permute-start.5 = (bf16[512,256]{1,0:T(8,128)(2,1)S(1)}, bf16[512,256]{1,0:T(8,128)(2,1)S(1)}, u32[]{:S(2)}, u32[]{:S(2)}) collective-permute-start(bf16[512,256]{1,0:T(8,128)(2,1)S(1)} %get-tuple-element.45), channel_id=1, source_target_pairs={{1,2},{3,4},{5,6},{7,8},{9,10},{11,12},{13,14},{2,1},{4,3},{6,5},{... | collective-permute-start | bytes 786440 | tf_op jit(solution)/shard_map/ppermute | solution.py:454
  52.7 0.0 collective-permute-done.7.refs_9_
  52.7 0.0 collective-permute-done.9.refs_11_
  52.7 0.0 collective-permute-done.8.refs_10_
  52.7 4.1 %settle0.1 = (bf16[512,1024]{1,0:T(8,128)(2,1)}, bf16[512,1024]{1,0:T(8,128)(2,1)}, bf16[512,1024]{1,0:T(8,128)(2,1)}, bf16[512,1024]{1,0:T(8,128)(2,1)}) custom-call(s32[4]{0:T(128)S(1)} %copy-done.4, s32[4]{0:T(128)S(1)} %copy-done.5, f32[512,256]{1,0:T(8,128)S(1)} %get-tuple-element.49.refs_0_.refs_2_, ...), custom_call_target="tpu_custom_call", output_to_operand_aliasing={{0}: (14, {}), {1}: (15, {})} | custom-call | bytes 5242880 | tf_op jit(solution)/shard_map/settle0/pallas_call | solution.py:422
  56.8 0.0 collective-permute-done.6.refs_2_
  56.8 1.6 %settle1.1 = (bf16[512,1024]{1,0:T(8,128)(2,1)}, bf16[512,1024]{1,0:T(8,128)(2,1)}, bf16[512,1024]{1,0:T(8,128)(2,1)}, bf16[512,1024]{1,0:T(8,128)(2,1)}) custom-call(s32[4]{0:T(128)S(1)} %copy-done.4, s32[4]{0:T(128)S(1)} %copy-done.5, ...), custom_call_target="tpu_custom_call", output_to_operand_aliasing={{0}: (5, {}), {1}: (6, {}), {2}: (7, {}), {3}: (8, {})} | custom-call | bytes 2097152 | tf_op jit(solution)/shard_map/settle1/pallas_call | solution.py:422
  58.3 2.9 %collective-permute-done.5.refs_2_ = bf16[512,256]{1,0:T(8,128)(2,1)S(1)} collective-permute-done((bf16[512,256]{1,0:T(8,128)(2,1)S(1)}, bf16[512,256]{1,0:T(8,128)(2,1)S(1)}, u32[]{:S(2)}, u32[]{:S(2)}) %collective-permute-start.5) | collective-permute-done | bytes 262176 | tf_op jit(solution)/shard_map/ppermute | solution.py:454
  61.2 2.0 %settle2.1 = (bf16[512,1024]{1,0:T(8,128)(2,1)}, bf16[512,1024]{1,0:T(8,128)(2,1)}, bf16[512,1024]{1,0:T(8,128)(2,1)}, bf16[512,1024]{1,0:T(8,128)(2,1)}) custom-call(s32[4]{0:T(128)S(1)} %copy-done.4, s32[4]{0:T(128)S(1)} %copy-done.5, ...), custom_call_target="tpu_custom_call", output_to_operand_aliasing={{0}: (5, {}), {1}: (6, {}), {2}: (7, {}), {3}: (8, {})} | custom-call | bytes 1048576 | tf_op jit(solution)/shard_map/settle2/pallas_call | solution.py:422
  (8 shorter events, 0.0 us)
Async XLA Ops:
  3.2 10.8 %collective-permute-start.1 = (bf16[528,256]{1,0:T(8,128)(2,1)}, bf16[528,256]{1,0:T(8,128)(2,1)S(1)}, u32[]{:S(2)}, u32[]{:S(2)}) collective-permute-start(bf16[528,256]{1,0:T(8,128)(2,1)} %get-tuple-element.35), channel_id=1, source_target_pairs={{0,1},{1,0},{2,3},{3,2},{4,5},{5,4},{6,7},{7,6},{8,9},{9,8},{10,11... | collective-permute-start | bytes 811016 | tf_op jit(solution)/shard_map/ppermute | solution.py:454
  3.9 11.2 %copy-start = (bf16[512,1024]{1,0:T(8,128)(2,1)S(1)}, bf16[512,1024]{1,0:T(8,128)(2,1)}, u32[]{:S(2)}) copy-start(bf16[512,1024]{1,0:T(8,128)(2,1)} %q.9) | copy-start | bytes 3145732
  3.9 11.2 %copy-start.1 = (bf16[512,1024]{1,0:T(8,128)(2,1)S(1)}, bf16[512,1024]{1,0:T(8,128)(2,1)}, u32[]{:S(2)}) copy-start(bf16[512,1024]{1,0:T(8,128)(2,1)} %k.9) | copy-start | bytes 3145732
  3.9 11.2 %copy-start.2 = (bf16[512,1024]{1,0:T(8,128)(2,1)S(1)}, bf16[512,1024]{1,0:T(8,128)(2,1)}, u32[]{:S(2)}) copy-start(bf16[512,1024]{1,0:T(8,128)(2,1)} %v.9) | copy-start | bytes 3145732
  3.9 11.2 %copy-start.3 = (bf16[512,1024]{1,0:T(8,128)(2,1)S(1)}, bf16[512,1024]{1,0:T(8,128)(2,1)}, u32[]{:S(2)}) copy-start(bf16[512,1024]{1,0:T(8,128)(2,1)} %g.9) | copy-start | bytes 3145732
  3.9 11.1 %collective-permute-start = (bf16[528,256]{1,0:T(8,128)(2,1)}, bf16[528,256]{1,0:T(8,128)(2,1)S(1)}, u32[]{:S(2)}, u32[]{:S(2)}) collective-permute-start(bf16[528,256]{1,0:T(8,128)(2,1)} %get-tuple-element.34.rest_0_), channel_id=1, source_target_pairs={{1,2},{3,4},{5,6},{7,8},{9,10},{11,12},{13,14},{2,1},{4,3},{6,5},{... | collective-permute-start | bytes 811016 | tf_op jit(solution)/shard_map/ppermute | solution.py:454
  10.3 4.8 %copy-start.4 = (s32[4]{0:T(128)S(1)}, s32[4]{0:T(128)}, u32[]{:S(2)}) copy-start(s32[4]{0:T(128)} %starts.15) | copy-start | bytes 52
  10.3 4.8 %copy-start.5 = (s32[4]{0:T(128)S(1)}, s32[4]{0:T(128)}, u32[]{:S(2)}) copy-start(s32[4]{0:T(128)} %ends.15) | copy-start | bytes 52
  10.3 16.7 %collective-permute-start.3 = (bf16[512,768]{1,0:T(8,128)(2,1)}, bf16[512,768]{1,0:T(8,128)(2,1)S(1)}, u32[]{:S(2)}, u32[]{:S(2)}) collective-permute-start(bf16[512,768]{1,0:T(8,128)(2,1)} %get-tuple-element.37), channel_id=1, source_target_pairs={{0,1},{1,0},{2,3},{3,2},{4,5},{5,4},{6,7},{7,6},{8,9},{9,8},{10,11... | collective-permute-start | bytes 2359304 | tf_op jit(solution)/shard_map/ppermute | solution.py:454
  10.8 16.3 %collective-permute-start.4 = (bf16[512,512]{1,0:T(8,128)(2,1)}, bf16[512,512]{1,0:T(8,128)(2,1)S(1)}, u32[]{:S(2)}, u32[]{:S(2)}) collective-permute-start(bf16[512,512]{1,0:T(8,128)(2,1)} %get-tuple-element.38), channel_id=1, source_target_pairs={{1,2},{3,4},{5,6},{7,8},{9,10},{11,12},{13,14},{2,1},{4,3},{6,5},{... | collective-permute-start | bytes 1572872 | tf_op jit(solution)/shard_map/ppermute | solution.py:454
  22.6 30.1 %collective-permute-start.7 = (bf16[512,256]{1,0:T(8,128)(2,1)S(1)}, bf16[512,256]{1,0:T(8,128)(2,1)S(1)}, u32[]{:S(2)}, u32[]{:S(2)}) collective-permute-start(bf16[512,256]{1,0:T(8,128)(2,1)S(1)} %get-tuple-element.51), channel_id=1, source_target_pairs={{0,1},{1,0},{2,3},{3,2},{4,5},{5,4},{6,7},{7,6},{8,9},{9,8},{10,11... | collective-permute-start | bytes 786440 | tf_op jit(solution)/shard_map/ppermute | solution.py:454
  23.1 18.7 %collective-permute-start.2 = (bf16[1024,256]{1,0:T(8,128)(2,1)S(1)}, bf16[1024,256]{1,0:T(8,128)(2,1)S(1)}, u32[]{:S(2)}, u32[]{:S(2)}) collective-permute-start(bf16[1024,256]{1,0:T(8,128)(2,1)S(1)} %get-tuple-element.36), channel_id=1, source_target_pairs={{1,2},{3,4},{5,6},{7,8},{9,10},{11,12},{13,14},{2,1},{4,3},{6,5},{... | collective-permute-start | bytes 1572872 | tf_op jit(solution)/shard_map/ppermute | solution.py:454
  38.2 18.6 %collective-permute-start.6 = (bf16[512,512]{1,0:T(8,128)(2,1)S(1)}, bf16[512,512]{1,0:T(8,128)(2,1)S(1)}, u32[]{:S(2)}, u32[]{:S(2)}) collective-permute-start(bf16[512,512]{1,0:T(8,128)(2,1)S(1)} %get-tuple-element.48), channel_id=1, source_target_pairs={{1,2},{3,4},{5,6},{7,8},{9,10},{11,12},{13,14},{2,1},{4,3},{6,5},{... | collective-permute-start | bytes 1572872 | tf_op jit(solution)/shard_map/ppermute | solution.py:454
  40.1 12.6 %collective-permute-start.8 = (bf16[512,512]{1,0:T(8,128)(2,1)S(1)}, bf16[512,512]{1,0:T(8,128)(2,1)S(1)}, u32[]{:S(2)}, u32[]{:S(2)}) collective-permute-start(bf16[512,512]{1,0:T(8,128)(2,1)S(1)} %get-tuple-element.52), channel_id=1, source_target_pairs={{0,1},{1,0},{2,3},{3,2},{4,5},{5,4},{6,7},{7,6},{8,9},{9,8},{10,11... | collective-permute-start | bytes 1572872 | tf_op jit(solution)/shard_map/ppermute | solution.py:454
  49.0 3.7 %collective-permute-start.9 = (bf16[512,256]{1,0:T(8,128)(2,1)S(1)}, bf16[512,256]{1,0:T(8,128)(2,1)S(1)}, u32[]{:S(2)}, u32[]{:S(2)}) collective-permute-start(bf16[512,256]{1,0:T(8,128)(2,1)S(1)} %get-tuple-element.53), channel_id=1, source_target_pairs={{0,1},{1,0},{2,3},{3,2},{4,5},{5,4},{6,7},{7,6},{8,9},{9,8},{10,11... | collective-permute-start | bytes 786440 | tf_op jit(solution)/shard_map/ppermute | solution.py:454
  50.7 10.5 %collective-permute-start.5 = (bf16[512,256]{1,0:T(8,128)(2,1)S(1)}, bf16[512,256]{1,0:T(8,128)(2,1)S(1)}, u32[]{:S(2)}, u32[]{:S(2)}) collective-permute-start(bf16[512,256]{1,0:T(8,128)(2,1)S(1)} %get-tuple-element.45), channel_id=1, source_target_pairs={{1,2},{3,4},{5,6},{7,8},{9,10},{11,12},{13,14},{2,1},{4,3},{6,5},{... | collective-permute-start | bytes 786440 | tf_op jit(solution)/shard_map/ppermute | solution.py:454
